TPU v7x, 32 devices: a whole 2x2x4 slice. The times are simulated.
32 devices in a mesh: groups: 2 (over x), rows: 16 (over z, y, core).
Axes of the slice: x: 2, y: 2, z: 4, core: 2. Of those that a mesh axis runs over, the one named last changes fastest.
Arguments:
- block_input: bfloat16 [512, 352, 512], P(('groups', 'rows')), parts along dimension 0, may hold values from -6 to 6
- first_pre: bfloat16 [512, 352, 128], P(('groups', 'rows')), parts along dimension 0, may hold values from -6 to 6
- second_pre: bfloat16 [512, 352, 128], P(('groups', 'rows')), parts along dimension 0, may hold values from -6 to 6
- output_pre: bfloat16 [512, 352, 512], P(('groups', 'rows')), parts along dimension 0, may hold values from -6 to 6
- output_grad: bfloat16 [512, 352, 512], P('groups', None, 'rows'), parts along dimension 0, may hold values from -6 to 6
- first_weight: bfloat16 [512, 128], replicated, may hold values from -0.25 to 0.25
- middle_weight: bfloat16 [3, 3, 128, 128], replicated, may hold values from -0.1875 to 0.1875
- last_weight: bfloat16 [128, 512], replicated, may hold values from -0.5 to 0.5
Outputs:
- input_grad: bfloat16 [512, 352, 512], P(('groups', 'rows')), parts along dimension 0
- first_weight_grad: float32 [1024, 128], P(('groups', 'rows')), parts along dimension 0
- middle_weight_grad: float32 [6, 3, 128, 128], P('groups'), parts along dimension 0
- last_weight_grad: float32 [256, 512], P('groups'), parts along dimension 0
There are 2 independent parts, one for each index of `groups`. A program takes and returns all parts, laid end to end along the dimension named above; an argument that names none is the same for every part. Nothing has to cross between parts.
All inputs are finite; a program needn't handle non-finite values.
Results may differ from a plain program's by a relative error of at most 0.0049.
Values may be sent and summed in bfloat16 or wider, within the bound.
No kernel may reach another device: no remote copies, remote signals or barrier semaphores. Data moves between devices by JAX's collectives and lax.ppermute only.
A program may use at most 128 MiB of HBM per device.

v0:
```python
import math
import jax
import jax.numpy as jnp
from jax import lax
from jax.sharding import PartitionSpec as P


def with_halo(value, sides, width):
    for axis, dim in sides:
        size, length = (lax.axis_size(axis), value.shape[dim])
        up = [(i, (i + 1) % size) for i in range(size - 1)]
        down = [(j, i) for i, j in up]
        last = lax.slice_in_dim(value, length - width, length, axis=dim)
        leading = lax.slice_in_dim(value, 0, width, axis=dim)
        before = lax.ppermute(last, axis, up)
        after = lax.ppermute(leading, axis, down)
        value = jnp.concatenate([before, value, after], axis=dim)
    return value


def contract_rows(left, right):
    return lax.dot_general(
        left, right, (((0,), (0,)), ((), ())), preferred_element_type=jnp.float32
    )


def shards(
    block_input,
    first_pre,
    second_pre,
    output_pre,
    output_grad,
    first_weight,
    middle_weight,
    last_weight,
):
    tile_rows, map_cols, channels = block_input.shape
    inner_width = first_pre.shape[2]
    pixels = tile_rows * map_cols
    factor = 1.0 / math.sqrt(pixels * lax.axis_size("rows"))
    spatial = lax.all_to_all(output_grad, "rows", split_axis=0, concat_axis=2, tiled=True)
    masked_out = jnp.where(output_pre > 0, spatial, jnp.zeros_like(spatial))
    second_act = jnp.maximum(second_pre, jnp.zeros_like(second_pre))
    first_act = jnp.maximum(first_pre, jnp.zeros_like(first_pre))
    out_flat = masked_out.reshape(pixels, channels)
    last_part = contract_rows(second_act.reshape(pixels, inner_width), out_flat)
    last_total = lax.psum(last_part, "rows")
    inner = lax.dot_general(
        out_flat, last_weight, (((1,), (1,)), ((), ())), preferred_element_type=jnp.float32
    )
    second_grad = jnp.where(second_pre.reshape(pixels, inner_width) > 0, inner, 0.0).astype(
        jnp.bfloat16
    )
    second_flat = second_grad
    second_grad = second_flat.reshape(tile_rows, map_cols, inner_width)
    act_ext = with_halo(first_act, (("rows", 0),), 1)
    act_padded = jnp.pad(act_ext, ((0, 0), (1, 1), (0, 0)))
    taps = []
    for row_tap in range(3):
        line = []
        for col_tap in range(3):
            window = act_padded[
                row_tap : row_tap + tile_rows, col_tap : col_tap + map_cols
            ].reshape(pixels, inner_width)
            line.append(contract_rows(window, second_flat))
        taps.append(jnp.stack(line))
    middle_part = jnp.stack(taps)
    grad_ext = with_halo(second_grad, (("rows", 0),), 1)
    grad_padded = jnp.pad(grad_ext, ((0, 0), (1, 1), (0, 0)))
    total = jnp.zeros((pixels, inner_width), jnp.float32)
    for row_tap in range(3):
        for col_tap in range(3):
            moved = grad_padded[
                2 - row_tap : 2 - row_tap + tile_rows, 2 - col_tap : 2 - col_tap + map_cols
            ].reshape(pixels, inner_width)
            total = total + lax.dot_general(
                moved,
                middle_weight[row_tap, col_tap],
                (((1,), (1,)), ((), ())),
                preferred_element_type=jnp.float32,
            )
    first_grad = jnp.where(first_pre.reshape(pixels, inner_width) > 0, total, 0.0).astype(
        jnp.bfloat16
    )
    input_flat = block_input.reshape(pixels, channels)
    first_wgrad = (
        lax.psum_scatter(
            contract_rows(input_flat, first_grad), "rows", scatter_dimension=0, tiled=True
        )
        * factor
    )
    back = lax.dot_general(
        first_grad, first_weight, (((1,), (1,)), ((), ())), preferred_element_type=jnp.float32
    )
    input_grad = (
        (back + out_flat.astype(jnp.float32))
        .astype(jnp.bfloat16)
        .reshape(tile_rows, map_cols, channels)
    )
    middle_total = lax.psum(middle_part, "rows")
    return (input_grad, first_wgrad, middle_total * factor, last_total * factor)


def solution(mesh):
    placed = (
        P(("groups", "rows"), None, None),
        P(("groups", "rows"), None, None),
        P(("groups", "rows"), None, None),
        P(("groups", "rows"), None, None),
        P("groups", None, "rows"),
        P(),
        P(),
        P(),
    )
    return jax.shard_map(
        shards,
        mesh=mesh,
        in_specs=placed,
        out_specs=(
            P(("groups", "rows"), None, None),
            P(("groups", "rows"), None),
            P("groups", None, None, None),
            P("groups", None),
        ),
        check_vma=False,
    )
```

profile of v0, /device:TPU:0, one launch (start us, length us, event | category | flops | bytes accessed | tf_op | source)
XLA Modules:
  0.0 376.6 jit_solution(985985323894171516)
XLA Ops:
  7.2 9.7 %copy.21 = bf16[256,352,32]{1,2,0:T(8,128)(2,1)} copy(bf16[256,352,32]{0,2,1:T(8,128)(2,1)} %param.12) | data formatting | bytes 11534336 | tf_op args[4]
  16.8 7.6 %all-to-all-start = ((bf16[256,352,32]{1,2,0:T(8,128)(2,1)}), bf16[256,352,32]{1,2,0:T(8,128)(2,1)}, u32[]{:S(2)}, u32[]{:S(2)}) async-start(bf16[256,352,32]{1,2,0:T(8,128)(2,1)} %copy.21), calls=%async_computation | async-start | bytes 12582912 | tf_op jit(solution)/shard_map/all_to_all | solution.py:41
  24.6 2.4 collective-permute-start.2
  27.0 1.3 collective-permute-start.3
  28.3 1.3 broadcast_compare_fusion.1
  29.6 1.3 broadcast_compare_fusion
  30.9 8.3 %copy.20 = bf16[16,352,512]{1,2,0:T(8,128)(2,1)} copy(bf16[16,352,512]{2,1,0:T(8,128)(2,1)} %param.11) | data formatting | bytes 11534336 | tf_op args[3]
  39.2 1.7 pad_maximum_fusion.1
  41.4 3.9 %fusion.33 = (bf16[16,352,128]{2,1,0:T(8,128)(2,1)}, bf16[16,352,128]{2,1,0:T(8,128)(2,1)}, bf16[16,352,128]{2,1,0:T(8,128)(2,1)}, bf16[16,352,128]{2,1,0:T(8,12...) fusion(bf16[18,354,128]{2,1,0:T(8,128)(2,1)S(1)} %select_maximum_fusion), kind=kLoop, calls=%fused_computation.73 | loop fusion | bytes 17301504 | tf_op jit(solution)/shard_map/slice | solution.py:62
  45.3 93.3 %all-to-all-done = bf16[256,352,32]{1,2,0:T(8,128)(2,1)} async-done(((bf16[256,352,32]{1,2,0:T(8,128)(2,1)}), bf16[256,352,32]{1,2,0:T(8,128)(2,1)}, u32[]{:S(2)}, u32[]{:S(2)}) %all-to-all-start) | async-done | bytes 5767200 | tf_op jit(solution)/shard_map/all_to_all | solution.py:41
  138.6 6.4 %copy.22 = bf16[16,352,16,32]{1,3,2,0:T(8,128)(2,1)} copy(bf16[16,352,16,32]{1,3,0,2:T(8,128)(2,1)} %bitcast.3) | data formatting | bytes 11534336 | tf_op jit(solution)/shard_map/all_to_all | solution.py:41
  145.0 8.0 %compare_select_fusion = bf16[16,352,512]{1,2,0:T(8,128)(2,1)} fusion(bf16[16,352,512]{1,2,0:T(8,128)(2,1)} %copy.20, bf16[16,352,16,32]{1,3,2,0:T(8,128)(2,1)} %copy.22), kind=kLoop, calls=%fused_computation | loop fusion | flops 5767168 | bytes 17301504 | tf_op jit(solution)/shard_map/jit(_where)/select_n | solution.py:42
  153.1 8.5 %copy.23 = bf16[16,352,512]{2,1,0:T(8,128)(2,1)} copy(bf16[16,352,512]{1,2,0:T(8,128)(2,1)} %compare_select_fusion) | data formatting | bytes 11534336 | tf_op jit(solution)/shard_map/jit(_where)/select_n | solution.py:42
  161.6 5.8 %fusion.8 = f32[128,512]{1,0:T(8,128)} fusion(bf16[16,352,512]{1,2,0:T(8,128)(2,1)} %compare_select_fusion, bf16[16,352,128]{2,1,0:T(8,128)(2,1)S(1)} %copy-done.12), kind=kOutput, calls=%fused_computation.28 | convolution fusion | flops 738918400 | bytes 7471104 | tf_op jit(solution)/shard_map/dot_general | solution.py:22
  167.5 1.7 fusion.3
  169.2 0.6 convolution_bitcast_fusion.4
  169.8 0.7 copy-done.9
  170.5 0.6 convolution_bitcast_fusion.6
  171.1 0.8 copy-done.8
  171.9 0.6 convolution_bitcast_fusion.7
  172.5 0.8 copy-done.7
  173.3 0.6 convolution_bitcast_fusion.9
  173.8 0.8 copy-done.4
  174.6 0.6 convolution_bitcast_fusion.8
  175.2 0.6 convolution_bitcast_fusion.5
  175.8 0.8 copy-done.6
  176.6 0.6 convolution_bitcast_fusion.1
  177.2 0.8 copy-done.5
  177.9 0.6 convolution_bitcast_fusion.3
  178.5 0.8 copy-done.3
  179.3 0.6 convolution_bitcast_fusion.2
  179.9 2.7 collective-permute-start
  182.6 1.3 collective-permute-start.1
  183.9 0.9 pad_maximum_fusion.4
  185.0 8.5 %collective-permute-done.1 = bf16[1,352,128]{2,1,0:T(8,128)(2,1)S(1)} collective-permute-done((bf16[1,352,128]{2,1,0:T(8,128)(2,1)S(1)}, bf16[1,352,128]{2,1,0:T(8,128)(2,1)S(1)}, u32[]{:S(2)}, u32[]{:S(2)}) %collective-permute-start.1) | collective-permute-done | bytes 90144 | tf_op jit(solution)/shard_map/ppermute | solution.py:16
  194.1 2.4 fusion.34
  198.3 0.6 convolution_add_fusion.4
  201.6 0.8 fusion.2
  202.9 0.7 slice-done.1
  203.6 1.0 convolution_bitcast_fusion
  204.6 0.8 copy.27
  205.5 6.8 %add_convert_fusion = bf16[5632,512]{1,0:T(8,128)(2,1)} fusion(bf16[5632,512]{1,0:T(8,128)(2,1)} %bitcast.124, bf16[5632,128]{1,0:T(8,128)(2,1)S(1)} %fusion.2, bf16[512,128]{1,0:T(8,128)(2,1)S(1)} %copy-done), kind=kOutput, calls=%fused_computation.1 | convolution fusion | flops 746848256 | bytes 13107200 | tf_op jit(solution)/shard_map/dot_general | solution.py:92
  212.3 97.3 %all-reduce.5.cloned.1.call-done = (f32[3,3,128,128]{3,2,1,0:T(8,128)}, f32[128,512]{1,0:T(8,128)}) async-done(((f32[3,3,128,128]{3,2,1,0:T(8,128)}, f32[128,512]{1,0:T(8,128)}), (f32[3,3,128,128]{3,2,1,0:T(8,128)}, f32[128,512]{1,0:T(8,128)})) %all-reduce.5.cloned.1.call-update) | async-done | bytes 851984 | tf_op jit(solution)/shard_map/psum | solution.py:100
  309.6 1.7 broadcast_multiply_fusion.1
  311.3 1.9 broadcast_multiply_fusion
  313.2 55.1 %reduce-scatter.4.cloned.1.call-done = f32[32,128]{1,0:T(8,128)} async-done(((f32[512,128]{1,0:T(8,128)}), f32[32,128]{1,0:T(8,128)}) %reduce-scatter.4.cloned.1.call-update) | async-done | bytes 16400
  368.2 0.8 copy.28
  369.1 0.7 copy.25
  (54 shorter events, 6.5 us)
Async XLA Ops:
  7.2 198.3 %copy-start = (bf16[512,128]{1,0:T(8,128)(2,1)S(1)}, bf16[512,128]{1,0:T(8,128)(2,1)}, u32[]{:S(2)}) copy-start(bf16[512,128]{1,0:T(8,128)(2,1)} %param.13) | copy-start | bytes 393220
  16.8 7.6 %copy-start.2 = (bf16[16,352,128]{2,1,0:T(8,128)(2,1)S(1)}, bf16[16,352,128]{2,1,0:T(8,128)(2,1)}, u32[]{:S(2)}) copy-start(bf16[16,352,128]{2,1,0:T(8,128)(2,1)} %param.9) | copy-start | bytes 4325380
  16.8 121.8 %all-to-all-start = ((bf16[256,352,32]{1,2,0:T(8,128)(2,1)}), bf16[256,352,32]{1,2,0:T(8,128)(2,1)}, u32[]{:S(2)}, u32[]{:S(2)}) async-start(bf16[256,352,32]{1,2,0:T(8,128)(2,1)} %copy.21), calls=%async_computation | async-start | bytes 12582912 | tf_op jit(solution)/shard_map/all_to_all | solution.py:41
  24.4 285.2 %all-reduce.5.cloned.1.call-start = ((), (), s32[]{:S(2)}) async-start(), calls=%async_computation.3 | async-start | bytes 1703936 | tf_op jit(solution)/shard_map/psum | solution.py:100
  24.6 5.0 %copy-start.11 = (bf16[16,352,128]{2,1,0:T(8,128)(2,1)S(1)}, bf16[16,352,128]{2,1,0:T(8,128)(2,1)}, u32[]{:S(2)}) copy-start(bf16[16,352,128]{2,1,0:T(8,128)(2,1)} %param.10) | copy-start | bytes 4325380
  24.6 14.6 %collective-permute-start.2 = (bf16[1,352,128]{2,1,0:T(8,128)(2,1)S(1)}, bf16[1,352,128]{2,1,0:T(8,128)(2,1)S(1)}, u32[]{:S(2)}, u32[]{:S(2)}) collective-permute-start(bf16[1,352,128]{2,1,0:T(8,128)(2,1)S(1)} %get-tuple-element.32), channel_id=1, source_target_pairs={{0,1},{1,2},{2,3},{3,4},{4,5},{5,6},{6,7},{7,8},{8,9},{9,10},{10,1... | collective-permute-start | bytes 270344 | tf_op jit(solution)/shard_map/ppermute | solution.py:15
  27.0 12.2 %collective-permute-start.3 = (bf16[1,352,128]{2,1,0:T(8,128)(2,1)S(1)}, bf16[1,352,128]{2,1,0:T(8,128)(2,1)S(1)}, u32[]{:S(2)}, u32[]{:S(2)}) collective-permute-start(bf16[1,352,128]{2,1,0:T(8,128)(2,1)S(1)} %get-tuple-element.33), channel_id=1, source_target_pairs={{1,0},{2,1},{3,2},{4,3},{5,4},{6,5},{7,6},{8,7},{9,8},{10,9},{11,1... | collective-permute-start | bytes 270344 | tf_op jit(solution)/shard_map/ppermute | solution.py:16
  153.1 8.5 %copy-start.12 = (bf16[16,352,128]{2,1,0:T(8,128)(2,1)S(1)}, bf16[16,352,128]{2,1,0:T(8,128)(2,1)}, u32[]{:S(2)}) copy-start(bf16[16,352,128]{2,1,0:T(8,128)(2,1)} %param.10) | copy-start | bytes 4325380
  161.6 5.8 %copy-start.1 = (bf16[16,352,512]{2,1,0:T(8,128)(2,1)S(1)}, bf16[16,352,512]{2,1,0:T(8,128)(2,1)}, u32[]{:S(2)}) copy-start(bf16[16,352,512]{2,1,0:T(8,128)(2,1)} %copy.23) | copy-start | bytes 17301508
  161.6 5.8 %copy-start.14 = (pred[16,352,128]{2,1,0:T(32,128)(4,1)S(1)}, pred[16,352,128]{2,1,0:T(32,128)(4,1)}, u32[]{:S(2)}) copy-start(pred[16,352,128]{2,1,0:T(32,128)(4,1)} %broadcast_compare_fusion) | copy-start | bytes 2162692
  161.6 5.8 %copy-start.16 = (bf16[128,512]{1,0:T(8,128)(2,1)S(1)}, bf16[128,512]{1,0:T(8,128)(2,1)}, u32[]{:S(2)}) copy-start(bf16[128,512]{1,0:T(8,128)(2,1)} %param.15) | copy-start | bytes 393220
  167.5 1.7 copy-start.10
  169.2 1.4 copy-start.9
  170.5 1.4 copy-start.8
  171.9 1.4 copy-start.7
  173.3 1.4 copy-start.4
  175.2 1.4 copy-start.6
  176.6 1.4 copy-start.5
  177.9 1.4 copy-start.3
  179.9 5.2 %collective-permute-start = (bf16[1,352,128]{2,1,0:T(8,128)(2,1)S(1)}, bf16[1,352,128]{2,1,0:T(8,128)(2,1)S(1)}, u32[]{:S(2)}, u32[]{:S(2)}) collective-permute-start(bf16[1,352,128]{2,1,0:T(8,128)(2,1)S(1)} %get-tuple-element.36), channel_id=1, source_target_pairs={{0,1},{1,2},{2,3},{3,4},{4,5},{5,6},{6,7},{7,8},{8,9},{9,10},{10,1... | collective-permute-start | bytes 270344 | tf_op jit(solution)/shard_map/ppermute | solution.py:15
  182.6 11.0 %collective-permute-start.1 = (bf16[1,352,128]{2,1,0:T(8,128)(2,1)S(1)}, bf16[1,352,128]{2,1,0:T(8,128)(2,1)S(1)}, u32[]{:S(2)}, u32[]{:S(2)}) collective-permute-start(bf16[1,352,128]{2,1,0:T(8,128)(2,1)S(1)} %get-tuple-element.37), channel_id=1, source_target_pairs={{1,0},{2,1},{3,2},{4,3},{5,4},{6,5},{7,6},{8,7},{9,8},{10,9},{11,1... | collective-permute-start | bytes 270344 | tf_op jit(solution)/shard_map/ppermute | solution.py:16
  184.8 183.4 %reduce-scatter.4.cloned.1.call-start = ((), (), s32[]{:S(2)}) async-start(), calls=%async_computation.2 | async-start | bytes 278528
  194.1 2.4 copy-start.15
  200.5 1.1 copy-start.13
  200.5 2.4 slice-start
  201.6 2.0 slice-start.1
Sparse Core Ops, SparseCore 0:
  184.9 124.6 all-reduce.4
  313.1 55.1 reduce-scatter.3
where the time goes:
time: 378 us; the launch traced here: 377 us
  waiting for transfers between devices  254 us (67%)
  local copies, waits for them, and re-layouts  48.8 us (13%)
  matrix products  25.6 us (7%)
  other arithmetic  18 us (5%)
  starting transfers between devices  15.5 us (4%)
  between operations  14.4 us (4%)
    psum x1, waiting for transfers between devices, shards(): middle_total = lax.psum(middle_part, 'rows')  97.3 us
    all_to_all x1, waiting for transfers between devices, shards(): lax.all_to_all(output_grad, 'rows', split_axis=0, concat_axis=2, tiled=True)  93.3 us
    unnamed x3, waiting for transfers between devices  55.1 us
    unnamed x43, local copies, waits for them, and re-layouts  27.6 us
    dot_general x11, matrix products, contract_rows(): lax.dot_general(left, right, (((0,), (0,)), ((), ())), preferred_element_...  12 us
    ppermute x2, waiting for transfers between devices, with_halo(): after = lax.ppermute(leading, axis, down)  8.54 us
    select_n x1, local copies, waits for them, and re-layouts, shards(): masked_out = jnp.where(output_pre > 0, spatial, jnp.zeros_like(spatial))  8.53 us
    select_n x1, other arithmetic, shards(): masked_out = jnp.where(output_pre > 0, spatial, jnp.zeros_like(spatial))  8.04 us
  transfers between devices with their start and end apart: 7, of which 4 were waited for; matrix products, arithmetic and copies ran while one was open for 10% of the time, Pallas kernels for 0%

commit v1 on v0

--- a/solution.py
+++ b/solution.py
@@ -3,6 +3,29 @@
 import jax.numpy as jnp
 from jax import lax
 from jax.sharding import PartitionSpec as P
+
+
+def in_blocks(x, dim, peers):
+    lengths = x.shape
+    pieces = x.reshape(*lengths[:dim], peers, lengths[dim] // peers, *lengths[dim + 1 :])
+    return jnp.moveaxis(pieces, dim, 0)
+
+
+def joined_along(pieces, dim):
+    pieces = jnp.moveaxis(pieces, 0, dim)
+    shape = pieces.shape
+    return pieces.reshape(*shape[:dim], shape[dim] * shape[dim + 1], *shape[dim + 2 :])
+
+
+def pairwise_exchange(x, axis, split_dim, concat_dim):
+    peers, here = (lax.axis_size(axis), lax.axis_index(axis))
+    tiles = in_blocks(x, split_dim, peers)
+    outs = [tiles[here]]
+    for step in range(1, peers):
+        sent = tiles[here ^ step]
+        outs.append(lax.ppermute(sent, axis, [(i, i ^ step) for i in range(peers)]))
+    tiles = jnp.stack(outs)[here ^ jnp.arange(peers)]
+    return joined_along(tiles, concat_dim)
 
 
 def with_halo(value, sides, width):
@@ -38,7 +61,7 @@
     inner_width = first_pre.shape[2]
     pixels = tile_rows * map_cols
     factor = 1.0 / math.sqrt(pixels * lax.axis_size("rows"))
-    spatial = lax.all_to_all(output_grad, "rows", split_axis=0, concat_axis=2, tiled=True)
+    spatial = pairwise_exchange(output_grad, "rows", 0, 2)
     masked_out = jnp.where(output_pre > 0, spatial, jnp.zeros_like(spatial))
     second_act = jnp.maximum(second_pre, jnp.zeros_like(second_pre))
     first_act = jnp.maximum(first_pre, jnp.zeros_like(first_pre))

time: 378 us -> 410 us (1.085)
  starting transfers between devices: 15.5 us -> 68.9 us
  waiting for transfers between devices: 254 us -> 209 us
  local copies, waits for them, and re-layouts: 48.8 us -> 72.8 us
    all_to_all x1 -> x0, waiting for transfers between devices: 93.3 us -> none  [shards(): lax.all_to_all(output_grad, 'rows', split_axis=0, concat_axis=2, tiled=True)]
    ppermute x0 -> x15, starting transfers between devices: none -> 61.1 us  [pairwise_exchange(): outs.append(lax.ppermute(sent, axis, [(i, i ^ step) for i in range(peers)]))]
    ppermute x0 -> x15, waiting for transfers between devices: none -> 49.6 us  [pairwise_exchange(): outs.append(lax.ppermute(sent, axis, [(i, i ^ step) for i in range(peers)]))]
    unnamed x43 -> x83, local copies, waits for them, and re-layouts: 27.6 us -> 40 us
    ppermute x2, waiting for transfers between devices: 8.54 us -> 0.88 us  [with_halo(): after = lax.ppermute(leading, axis, down)]
    all_to_all x1 -> x0, starting transfers between devices: 7.56 us -> none  [shards(): lax.all_to_all(output_grad, 'rows', split_axis=0, concat_axis=2, tiled=True)]
    gather x0 -> x1, local copies, waits for them, and re-layouts: none -> 6.82 us  [pairwise_exchange(): tiles = jnp.stack(outs)[here ^ jnp.arange(peers)]]
    all_to_all x1 -> x0, local copies, waits for them, and re-layouts: 6.43 us -> none  [shards(): lax.all_to_all(output_grad, 'rows', split_axis=0, concat_axis=2, tiled=True)]
  transfers between devices with their start and end apart: 7 -> 21, of which waited for: 4 -> 7; matrix products, arithmetic and copies ran while one was open for 10% -> 14% of each run, Pallas kernels for 0% -> 0%
where the time goes in v1:
time: 410 us; the launch traced here: 409 us
  waiting for transfers between devices  209 us (51%)
  local copies, waits for them, and re-layouts  72.8 us (18%)
  starting transfers between devices  68.9 us (17%)
  matrix products  25.6 us (6%)
  other arithmetic  18.3 us (4%)
  between operations  14.6 us (4%)
    psum x1, waiting for transfers between devices, shards(): middle_total = lax.psum(middle_part, 'rows')  103 us
    ppermute x15, starting transfers between devices, pairwise_exchange(): outs.append(lax.ppermute(sent, axis, [(i, i ^ step) for i in range(peers)]))  61.1 us
    unnamed x3, waiting for transfers between devices  55.1 us
    ppermute x15, waiting for transfers between devices, pairwise_exchange(): outs.append(lax.ppermute(sent, axis, [(i, i ^ step) for i in range(peers)]))  49.6 us
    unnamed x83, local copies, waits for them, and re-layouts  40 us
    dot_general x11, matrix products, contract_rows(): lax.dot_general(left, right, (((0,), (0,)), ((), ())), preferred_element_...  12 us
    select_n x1, local copies, waits for them, and re-layouts, shards(): masked_out = jnp.where(output_pre > 0, spatial, jnp.zeros_like(spatial))  8.53 us
  transfers between devices with their start and end apart: 21, of which 7 were waited for; matrix products, arithmetic and copies ran while one was open for 14% of the time, Pallas kernels for 0%

profile of v1, /device:TPU:0, one launch (start us, length us, event | category | flops | bytes accessed | tf_op | source)
XLA Modules:
  0.0 409.0 jit_solution(745274926851184551)
XLA Ops:
  7.3 9.7 %copy.21 = bf16[256,352,32]{1,2,0:T(8,128)(2,1)} copy(bf16[256,352,32]{0,2,1:T(8,128)(2,1)} %param.12) | data formatting | bytes 11534336 | tf_op args[4]
  17.0 5.4 %dynamic-slice_bitcast_fusion = (bf16[16,352,32]{1,2,0:T(8,128)(2,1)S(1)}, bf16[16,352,32]{1,2,0:T(8,128)(2,1)}, bf16[16,352,32]{1,2,0:T(8,128)(2,1)}, bf16[16,3...) fusion(bf16[16,16,352,32]{2,3,1,0:T(8,128)(2,1)} %bitcast.188, ...), kind=kLoop, calls=%fused_computation.60 | loop fusion | bytes 12025920 | tf_op jit(solution)/shard_map/squeeze | solution.py:25
  22.9 2.6 collective-permute-start.1
  26.4 2.0 collective-permute-start.17
  28.5 1.3 collective-permute-start.18
  29.8 1.3 broadcast_compare_fusion.1
  31.1 8.4 %copy.20 = bf16[16,352,512]{1,2,0:T(8,128)(2,1)} copy(bf16[16,352,512]{2,1,0:T(8,128)(2,1)} %param.11) | data formatting | bytes 11534336 | tf_op args[3]
  39.5 1.3 broadcast_compare_fusion
  40.8 5.0 %collective-permute-start.3 = (bf16[16,352,32]{1,2,0:T(8,128)(2,1)S(1)}, bf16[16,352,32]{1,2,0:T(8,128)(2,1)S(1)}, u32[]{:S(2)}, u32[]{:S(2)}) collective-permute-start(bf16[16,352,32]{1,2,0:T(8,128)(2,1)S(1)} %copy-done.27), channel_id=1, source_target_pairs={{0,4},{1,5},{2,6},{3,7},{4,0},{5,1},{6,2},{7,3},{8,12},{9,13},{10,... | collective-permute-start | bytes 1081352 | tf_op jit(solution)/shard_map/ppermute | solution.py:26
  45.8 1.4 collective-permute-start.4
  47.1 1.3 select_maximum_fusion
  48.5 4.0 fusion.34
  52.5 2.9 pad_maximum_fusion.1
  55.4 2.0 collective-permute-start.5
  57.4 1.8 bitcast_dynamic-update-slice_fusion.14
  59.2 1.4 collective-permute-start.6
  60.6 1.8 bitcast_dynamic-update-slice_fusion.13
  62.4 1.7 collective-permute-start.7
  64.1 1.8 bitcast_dynamic-update-slice_fusion.12
  66.7 0.8 bitcast_dynamic-update-slice_fusion.11
  67.6 2.8 collective-permute-start.9
  71.2 19.8 %collective-permute-done.5 = bf16[16,352,32]{1,2,0:T(8,128)(2,1)S(1)} collective-permute-done((bf16[16,352,32]{1,2,0:T(8,128)(2,1)S(1)}, bf16[16,352,32]{1,2,0:T(8,128)(2,1)S(1)}, u32[]{:S(2)}, u32[]{:S(2)}) %collective-permute-start.5) | collective-permute-done | bytes 360480 | tf_op jit(solution)/shard_map/ppermute | solution.py:26
  92.2 2.8 collective-permute-start.11
  95.8 3.7 collective-permute-start.12
  100.4 35.9 %collective-permute-start.13 = (bf16[16,352,32]{1,2,0:T(8,128)(2,1)S(1)}, bf16[16,352,32]{1,2,0:T(8,128)(2,1)S(1)}, u32[]{:S(2)}, u32[]{:S(2)}) collective-permute-start(bf16[16,352,32]{1,2,0:T(8,128)(2,1)S(1)} %copy-done.17), channel_id=1, source_target_pairs={{0,14},{1,15},{2,12},{3,13},{4,10},{5,11},{6,8},{7,9},{8,6},{9,7},... | collective-permute-start | bytes 1081352 | tf_op jit(solution)/shard_map/ppermute | solution.py:26
  137.1 15.2 %collective-permute-done.9 = bf16[16,352,32]{1,2,0:T(8,128)(2,1)S(1)} collective-permute-done((bf16[16,352,32]{1,2,0:T(8,128)(2,1)S(1)}, bf16[16,352,32]{1,2,0:T(8,128)(2,1)S(1)}, u32[]{:S(2)}, u32[]{:S(2)}) %collective-permute-start.9) | collective-permute-done | bytes 360480 | tf_op jit(solution)/shard_map/ppermute | solution.py:26
  153.4 14.3 %collective-permute-done.10 = bf16[16,352,32]{1,2,0:T(8,128)(2,1)S(1)} collective-permute-done((bf16[16,352,32]{1,2,0:T(8,128)(2,1)S(1)}, bf16[16,352,32]{1,2,0:T(8,128)(2,1)S(1)}, u32[]{:S(2)}, u32[]{:S(2)}) %collective-permute-start.10) | collective-permute-done | bytes 360480 | tf_op jit(solution)/shard_map/ppermute | solution.py:26
  170.0 0.8 bitcast_dynamic-update-slice_fusion.1
  170.9 0.8 bitcast_dynamic-update-slice_fusion
  171.7 6.8 %gather_fusion = bf16[16,16,352,32]{2,3,1,0:T(8,128)(2,1)} fusion(bf16[16,16,352,32]{2,3,1,0:T(8,128)(2,1)} %bitcast_dynamic-update-slice_fusion, s32[1024]{0:T(1024)S(1)} %pad_clamp_fusion), kind=kCustom, calls=%fused_computation | custom fusion | bytes 11534400 | tf_op jit(solution)/shard_map/gather | solution.py:27
  178.5 3.8 copy.22
  182.3 6.3 %compare_select_fusion = bf16[16,352,512]{1,2,0:T(8,128)(2,1)} fusion(bf16[16,352,512]{1,2,0:T(8,128)(2,1)} %copy.20, bf16[16,352,16,32]{1,3,2,0:T(8,128)(2,1)S(1)} %copy.22), kind=kLoop, calls=%fused_computation.1 | loop fusion | flops 5767168 | bytes 17301504 | tf_op jit(solution)/shard_map/jit(_where)/select_n | solution.py:65
  188.6 8.5 %copy.23 = bf16[16,352,512]{2,1,0:T(8,128)(2,1)} copy(bf16[16,352,512]{1,2,0:T(8,128)(2,1)} %compare_select_fusion) | data formatting | bytes 11534336 | tf_op jit(solution)/shard_map/jit(_where)/select_n | solution.py:65
  197.1 5.8 %fusion.8 = f32[128,512]{1,0:T(8,128)} fusion(bf16[16,352,512]{1,2,0:T(8,128)(2,1)} %compare_select_fusion, bf16[16,352,128]{2,1,0:T(8,128)(2,1)S(1)} %copy-done.14), kind=kOutput, calls=%fused_computation.29 | convolution fusion | flops 738918400 | bytes 7471104 | tf_op jit(solution)/shard_map/dot_general | solution.py:45
  203.0 1.7 fusion.3
  213.5 3.1 collective-permute-start.15
  216.6 1.3 collective-permute-start.16
  218.0 0.9 pad_maximum_fusion.4
  218.9 0.9 collective-permute-done.16
  220.3 2.6 fusion.35
  230.0 1.0 convolution_bitcast_fusion
  231.1 0.8 copy.27
  231.9 6.8 %add_convert_fusion = bf16[5632,512]{1,0:T(8,128)(2,1)} fusion(bf16[5632,512]{1,0:T(8,128)(2,1)} %bitcast.186, bf16[5632,128]{1,0:T(8,128)(2,1)S(1)} %fusion.2, bf16[512,128]{1,0:T(8,128)(2,1)S(1)} %copy-done), kind=kOutput, calls=%fused_computation.2 | convolution fusion | flops 746848256 | bytes 13107200 | tf_op jit(solution)/shard_map/dot_general | solution.py:115
  238.8 103.2 %all-reduce.5.cloned.1.call-done = (f32[3,3,128,128]{3,2,1,0:T(8,128)}, f32[128,512]{1,0:T(8,128)}) async-done(((f32[3,3,128,128]{3,2,1,0:T(8,128)}, f32[128,512]{1,0:T(8,128)}), (f32[3,3,128,128]{3,2,1,0:T(8,128)}, f32[128,512]{1,0:T(8,128)})) %all-reduce.5.cloned.1.call-update) | async-done | bytes 851984 | tf_op jit(solution)/shard_map/psum | solution.py:123
  342.0 1.7 broadcast_multiply_fusion.1
  343.7 1.9 broadcast_multiply_fusion
  345.6 55.1 %reduce-scatter.4.cloned.1.call-done = f32[32,128]{1,0:T(8,128)} async-done(((f32[512,128]{1,0:T(8,128)}), f32[32,128]{1,0:T(8,128)}) %reduce-scatter.4.cloned.1.call-update) | async-done | bytes 16400
  400.6 0.8 copy.28
  (127 shorter events, 27.3 us)
Async XLA Ops:
  7.2 224.7 %copy-start = (bf16[512,128]{1,0:T(8,128)(2,1)S(1)}, bf16[512,128]{1,0:T(8,128)(2,1)}, u32[]{:S(2)}) copy-start(bf16[512,128]{1,0:T(8,128)(2,1)} %param.13) | copy-start | bytes 393220
  7.2 334.8 %all-reduce.5.cloned.1.call-start = ((), (), s32[]{:S(2)}) async-start(), calls=%async_computation.2 | async-start | bytes 1703936 | tf_op jit(solution)/shard_map/psum | solution.py:123
  17.0 8.6 %copy-start.4 = (bf16[16,352,128]{2,1,0:T(8,128)(2,1)S(1)}, bf16[16,352,128]{2,1,0:T(8,128)(2,1)}, u32[]{:S(2)}) copy-start(bf16[16,352,128]{2,1,0:T(8,128)(2,1)} %param.9) | copy-start | bytes 4325380
  22.4 33.0 %collective-permute-start = (bf16[16,352,32]{1,2,0:T(8,128)(2,1)}, bf16[16,352,32]{1,2,0:T(8,128)(2,1)}, u32[]{:S(2)}, u32[]{:S(2)}) collective-permute-start(bf16[16,352,32]{1,2,0:T(8,128)(2,1)} %get-tuple-element.32), channel_id=1, source_target_pairs={{0,1},{1,0},{2,3},{3,2},{4,5},{5,4},{6,7},{7,6},{8,9},{9,8},{10,11... | collective-permute-start | bytes 1081352 | tf_op jit(solution)/shard_map/ppermute | solution.py:26
  22.9 36.2 %collective-permute-start.1 = (bf16[16,352,32]{1,2,0:T(8,128)(2,1)}, bf16[16,352,32]{1,2,0:T(8,128)(2,1)}, u32[]{:S(2)}, u32[]{:S(2)}) collective-permute-start(bf16[16,352,32]{1,2,0:T(8,128)(2,1)} %get-tuple-element.31), channel_id=1, source_target_pairs={{0,2},{1,3},{2,0},{3,1},{4,6},{5,7},{6,4},{7,5},{8,10},{9,11},{10,... | collective-permute-start | bytes 1081352 | tf_op jit(solution)/shard_map/ppermute | solution.py:26
  25.5 36.9 %collective-permute-start.2 = (bf16[16,352,32]{1,2,0:T(8,128)(2,1)}, bf16[16,352,32]{1,2,0:T(8,128)(2,1)}, u32[]{:S(2)}, u32[]{:S(2)}) collective-permute-start(bf16[16,352,32]{1,2,0:T(8,128)(2,1)} %get-tuple-element.30), channel_id=1, source_target_pairs={{0,3},{1,2},{2,1},{3,0},{4,7},{5,6},{6,5},{7,4},{8,11},{9,10},{10,... | collective-permute-start | bytes 1081352 | tf_op jit(solution)/shard_map/ppermute | solution.py:26
  25.7 26.8 %copy-start.2 = (bf16[16,352,128]{2,1,0:T(8,128)(2,1)}, bf16[16,352,128]{2,1,0:T(8,128)(2,1)S(1)}, u32[]{:S(2)}) copy-start(bf16[16,352,128]{2,1,0:T(8,128)(2,1)S(1)} %broadcast_maximum_fusion) | copy-start | bytes 4325380
  26.4 14.4 %collective-permute-start.17 = (bf16[1,352,128]{2,1,0:T(8,128)(2,1)}, bf16[1,352,128]{2,1,0:T(8,128)(2,1)S(1)}, u32[]{:S(2)}, u32[]{:S(2)}) collective-permute-start(bf16[1,352,128]{2,1,0:T(8,128)(2,1)} %get-tuple-element.48), channel_id=1, source_target_pairs={{0,1},{1,2},{2,3},{3,4},{4,5},{5,6},{6,7},{7,8},{8,9},{9,10},{10,1... | collective-permute-start | bytes 270344 | tf_op jit(solution)/shard_map/ppermute | solution.py:38
  28.5 17.3 %collective-permute-start.18 = (bf16[1,352,128]{2,1,0:T(8,128)(2,1)}, bf16[1,352,128]{2,1,0:T(8,128)(2,1)}, u32[]{:S(2)}, u32[]{:S(2)}) collective-permute-start(bf16[1,352,128]{2,1,0:T(8,128)(2,1)} %get-tuple-element.49), channel_id=1, source_target_pairs={{1,0},{2,1},{3,2},{4,3},{5,4},{6,5},{7,6},{8,7},{9,8},{10,9},{11,1... | collective-permute-start | bytes 270344 | tf_op jit(solution)/shard_map/ppermute | solution.py:39
  31.1 8.4 %copy-start.13 = (bf16[16,352,128]{2,1,0:T(8,128)(2,1)S(1)}, bf16[16,352,128]{2,1,0:T(8,128)(2,1)}, u32[]{:S(2)}) copy-start(bf16[16,352,128]{2,1,0:T(8,128)(2,1)} %param.10) | copy-start | bytes 4325380
  39.5 6.3 %copy-start.26 = (bf16[16,352,32]{1,2,0:T(8,128)(2,1)S(1)}, bf16[16,352,32]{1,2,0:T(8,128)(2,1)}, u32[]{:S(2)}) copy-start(bf16[16,352,32]{1,2,0:T(8,128)(2,1)} %get-tuple-element.28) | copy-start | bytes 1081348
  40.8 25.1 %collective-permute-start.3 = (bf16[16,352,32]{1,2,0:T(8,128)(2,1)S(1)}, bf16[16,352,32]{1,2,0:T(8,128)(2,1)S(1)}, u32[]{:S(2)}, u32[]{:S(2)}) collective-permute-start(bf16[16,352,32]{1,2,0:T(8,128)(2,1)S(1)} %copy-done.27), channel_id=1, source_target_pairs={{0,4},{1,5},{2,6},{3,7},{4,0},{5,1},{6,2},{7,3},{8,12},{9,13},{10,... | collective-permute-start | bytes 1081352 | tf_op jit(solution)/shard_map/ppermute | solution.py:26
  45.8 21.8 %collective-permute-start.4 = (bf16[16,352,32]{1,2,0:T(8,128)(2,1)S(1)}, bf16[16,352,32]{1,2,0:T(8,128)(2,1)S(1)}, u32[]{:S(2)}, u32[]{:S(2)}) collective-permute-start(bf16[16,352,32]{1,2,0:T(8,128)(2,1)S(1)} %copy-done.26), channel_id=1, source_target_pairs={{0,5},{1,4},{2,7},{3,6},{4,1},{5,0},{6,3},{7,2},{8,13},{9,12},{10,... | collective-permute-start | bytes 1081352 | tf_op jit(solution)/shard_map/ppermute | solution.py:26
  52.5 2.9 copy-start.25
  52.5 6.6 %copy-start.24 = (bf16[16,352,32]{1,2,0:T(8,128)(2,1)S(1)}, bf16[16,352,32]{1,2,0:T(8,128)(2,1)}, u32[]{:S(2)}) copy-start(bf16[16,352,32]{1,2,0:T(8,128)(2,1)} %get-tuple-element.26) | copy-start | bytes 1081348
  52.5 9.9 %copy-start.23 = (bf16[16,352,32]{1,2,0:T(8,128)(2,1)S(1)}, bf16[16,352,32]{1,2,0:T(8,128)(2,1)}, u32[]{:S(2)}) copy-start(bf16[16,352,32]{1,2,0:T(8,128)(2,1)} %get-tuple-element.25) | copy-start | bytes 1081348
  55.4 10.5 %copy-start.22 = (bf16[16,352,32]{1,2,0:T(8,128)(2,1)S(1)}, bf16[16,352,32]{1,2,0:T(8,128)(2,1)}, u32[]{:S(2)}) copy-start(bf16[16,352,32]{1,2,0:T(8,128)(2,1)} %get-tuple-element.24) | copy-start | bytes 1081348
  55.4 12.2 %copy-start.21 = (bf16[16,352,32]{1,2,0:T(8,128)(2,1)S(1)}, bf16[16,352,32]{1,2,0:T(8,128)(2,1)}, u32[]{:S(2)}) copy-start(bf16[16,352,32]{1,2,0:T(8,128)(2,1)} %get-tuple-element.23) | copy-start | bytes 1081348
  55.4 35.6 %collective-permute-start.5 = (bf16[16,352,32]{1,2,0:T(8,128)(2,1)S(1)}, bf16[16,352,32]{1,2,0:T(8,128)(2,1)S(1)}, u32[]{:S(2)}, u32[]{:S(2)}) collective-permute-start(bf16[16,352,32]{1,2,0:T(8,128)(2,1)S(1)} %copy-done.25), channel_id=1, source_target_pairs={{0,6},{1,7},{2,4},{3,5},{4,2},{5,3},{6,0},{7,1},{8,14},{9,15},{10,... | collective-permute-start | bytes 1081352 | tf_op jit(solution)/shard_map/ppermute | solution.py:26
  59.2 31.8 %copy-start.20 = (bf16[16,352,32]{1,2,0:T(8,128)(2,1)S(1)}, bf16[16,352,32]{1,2,0:T(8,128)(2,1)}, u32[]{:S(2)}) copy-start(bf16[16,352,32]{1,2,0:T(8,128)(2,1)} %get-tuple-element.22) | copy-start | bytes 1081348
  59.2 33.0 %collective-permute-start.6 = (bf16[16,352,32]{1,2,0:T(8,128)(2,1)S(1)}, bf16[16,352,32]{1,2,0:T(8,128)(2,1)S(1)}, u32[]{:S(2)}, u32[]{:S(2)}) collective-permute-start(bf16[16,352,32]{1,2,0:T(8,128)(2,1)S(1)} %copy-done.24), channel_id=1, source_target_pairs={{0,7},{1,6},{2,5},{3,4},{4,3},{5,2},{6,1},{7,0},{8,15},{9,14},{10,... | collective-permute-start | bytes 1081352 | tf_op jit(solution)/shard_map/ppermute | solution.py:26
  62.4 29.8 %copy-start.19 = (bf16[16,352,32]{1,2,0:T(8,128)(2,1)S(1)}, bf16[16,352,32]{1,2,0:T(8,128)(2,1)}, u32[]{:S(2)}) copy-start(bf16[16,352,32]{1,2,0:T(8,128)(2,1)} %get-tuple-element.21) | copy-start | bytes 1081348
  62.4 33.4 %collective-permute-start.7 = (bf16[16,352,32]{1,2,0:T(8,128)(2,1)S(1)}, bf16[16,352,32]{1,2,0:T(8,128)(2,1)S(1)}, u32[]{:S(2)}, u32[]{:S(2)}) collective-permute-start(bf16[16,352,32]{1,2,0:T(8,128)(2,1)S(1)} %copy-done.23), channel_id=1, source_target_pairs={{0,8},{1,9},{2,10},{3,11},{4,12},{5,13},{6,14},{7,15},{8,0},{9,1},... | collective-permute-start | bytes 1081352 | tf_op jit(solution)/shard_map/ppermute | solution.py:26
  65.9 29.9 %copy-start.18 = (bf16[16,352,32]{1,2,0:T(8,128)(2,1)S(1)}, bf16[16,352,32]{1,2,0:T(8,128)(2,1)}, u32[]{:S(2)}) copy-start(bf16[16,352,32]{1,2,0:T(8,128)(2,1)} %get-tuple-element.20) | copy-start | bytes 1081348
  65.9 34.4 %collective-permute-start.8 = (bf16[16,352,32]{1,2,0:T(8,128)(2,1)S(1)}, bf16[16,352,32]{1,2,0:T(8,128)(2,1)S(1)}, u32[]{:S(2)}, u32[]{:S(2)}) collective-permute-start(bf16[16,352,32]{1,2,0:T(8,128)(2,1)S(1)} %copy-done.22), channel_id=1, source_target_pairs={{0,9},{1,8},{2,11},{3,10},{4,13},{5,12},{6,15},{7,14},{8,1},{9,0},... | collective-permute-start | bytes 1081352 | tf_op jit(solution)/shard_map/ppermute | solution.py:26
  67.6 32.8 %copy-start.17 = (bf16[16,352,32]{1,2,0:T(8,128)(2,1)S(1)}, bf16[16,352,32]{1,2,0:T(8,128)(2,1)}, u32[]{:S(2)}) copy-start(bf16[16,352,32]{1,2,0:T(8,128)(2,1)} %get-tuple-element.19) | copy-start | bytes 1081348
  67.6 84.6 %collective-permute-start.9 = (bf16[16,352,32]{1,2,0:T(8,128)(2,1)S(1)}, bf16[16,352,32]{1,2,0:T(8,128)(2,1)S(1)}, u32[]{:S(2)}, u32[]{:S(2)}) collective-permute-start(bf16[16,352,32]{1,2,0:T(8,128)(2,1)S(1)} %copy-done.21), channel_id=1, source_target_pairs={{0,10},{1,11},{2,8},{3,9},{4,14},{5,15},{6,12},{7,13},{8,2},{9,3},... | collective-permute-start | bytes 1081352 | tf_op jit(solution)/shard_map/ppermute | solution.py:26
  91.0 76.7 %collective-permute-start.10 = (bf16[16,352,32]{1,2,0:T(8,128)(2,1)S(1)}, bf16[16,352,32]{1,2,0:T(8,128)(2,1)S(1)}, u32[]{:S(2)}, u32[]{:S(2)}) collective-permute-start(bf16[16,352,32]{1,2,0:T(8,128)(2,1)S(1)} %copy-done.20), channel_id=1, source_target_pairs={{0,11},{1,10},{2,9},{3,8},{4,15},{5,14},{6,13},{7,12},{8,3},{9,2},... | collective-permute-start | bytes 1081352 | tf_op jit(solution)/shard_map/ppermute | solution.py:26
  92.2 76.3 %collective-permute-start.11 = (bf16[16,352,32]{1,2,0:T(8,128)(2,1)S(1)}, bf16[16,352,32]{1,2,0:T(8,128)(2,1)S(1)}, u32[]{:S(2)}, u32[]{:S(2)}) collective-permute-start(bf16[16,352,32]{1,2,0:T(8,128)(2,1)S(1)} %copy-done.19), channel_id=1, source_target_pairs={{0,12},{1,13},{2,14},{3,15},{4,8},{5,9},{6,10},{7,11},{8,4},{9,5},... | collective-permute-start | bytes 1081352 | tf_op jit(solution)/shard_map/ppermute | solution.py:26
  95.8 73.4 %collective-permute-start.12 = (bf16[16,352,32]{1,2,0:T(8,128)(2,1)S(1)}, bf16[16,352,32]{1,2,0:T(8,128)(2,1)S(1)}, u32[]{:S(2)}, u32[]{:S(2)}) collective-permute-start(bf16[16,352,32]{1,2,0:T(8,128)(2,1)S(1)} %copy-done.18), channel_id=1, source_target_pairs={{0,13},{1,12},{2,15},{3,14},{4,9},{5,8},{6,11},{7,10},{8,5},{9,4},... | collective-permute-start | bytes 1081352 | tf_op jit(solution)/shard_map/ppermute | solution.py:26
  100.4 69.7 %collective-permute-start.13 = (bf16[16,352,32]{1,2,0:T(8,128)(2,1)S(1)}, bf16[16,352,32]{1,2,0:T(8,128)(2,1)S(1)}, u32[]{:S(2)}, u32[]{:S(2)}) collective-permute-start(bf16[16,352,32]{1,2,0:T(8,128)(2,1)S(1)} %copy-done.17), channel_id=1, source_target_pairs={{0,14},{1,15},{2,12},{3,13},{4,10},{5,11},{6,8},{7,9},{8,6},{9,7},... | collective-permute-start | bytes 1081352 | tf_op jit(solution)/shard_map/ppermute | solution.py:26
  152.2 18.6 %collective-permute-start.14 = (bf16[16,352,32]{1,2,0:T(8,128)(2,1)S(1)}, bf16[16,352,32]{1,2,0:T(8,128)(2,1)S(1)}, u32[]{:S(2)}, u32[]{:S(2)}) collective-permute-start(bf16[16,352,32]{1,2,0:T(8,128)(2,1)S(1)} %get-tuple-element.18), channel_id=1, source_target_pairs={{0,15},{1,14},{2,13},{3,12},{4,11},{5,10},{6,9},{7,8},{8,7},{9,6},... | collective-permute-start | bytes 1081352 | tf_op jit(solution)/shard_map/ppermute | solution.py:26
  188.6 8.5 %copy-start.14 = (bf16[16,352,128]{2,1,0:T(8,128)(2,1)S(1)}, bf16[16,352,128]{2,1,0:T(8,128)(2,1)}, u32[]{:S(2)}) copy-start(bf16[16,352,128]{2,1,0:T(8,128)(2,1)} %param.10) | copy-start | bytes 4325380
  197.1 5.9 %copy-start.1 = (bf16[16,352,512]{2,1,0:T(8,128)(2,1)S(1)}, bf16[16,352,512]{2,1,0:T(8,128)(2,1)}, u32[]{:S(2)}) copy-start(bf16[16,352,512]{2,1,0:T(8,128)(2,1)} %copy.23) | copy-start | bytes 17301508
  197.1 5.9 %copy-start.16 = (pred[16,352,128]{2,1,0:T(32,128)(4,1)S(1)}, pred[16,352,128]{2,1,0:T(32,128)(4,1)}, u32[]{:S(2)}) copy-start(pred[16,352,128]{2,1,0:T(32,128)(4,1)} %broadcast_compare_fusion) | copy-start | bytes 2162692
  197.1 5.8 %copy-start.29 = (bf16[128,512]{1,0:T(8,128)(2,1)S(1)}, bf16[128,512]{1,0:T(8,128)(2,1)}, u32[]{:S(2)}) copy-start(bf16[128,512]{1,0:T(8,128)(2,1)} %param.15) | copy-start | bytes 393220
  203.0 1.7 copy-start.12
  205.3 1.5 copy-start.10
  207.4 1.5 copy-start.6
  209.4 1.5 copy-start.8
  210.6 1.4 copy-start.7
  211.5 1.5 copy-start.5
  213.5 5.4 %collective-permute-start.15 = (bf16[1,352,128]{2,1,0:T(8,128)(2,1)S(1)}, bf16[1,352,128]{2,1,0:T(8,128)(2,1)S(1)}, u32[]{:S(2)}, u32[]{:S(2)}) collective-permute-start(bf16[1,352,128]{2,1,0:T(8,128)(2,1)S(1)} %get-tuple-element.52), channel_id=1, source_target_pairs={{0,1},{1,2},{2,3},{3,4},{4,5},{5,6},{6,7},{7,8},{8,9},{9,10},{10,1... | collective-permute-start | bytes 270344 | tf_op jit(solution)/shard_map/ppermute | solution.py:38
  216.6 3.2 collective-permute-start.16
  218.9 181.8 %reduce-scatter.4.cloned.1.call-start = ((), (), s32[]{:S(2)}) async-start(), calls=%async_computation.1 | async-start | bytes 278528
  220.3 2.6 copy-start.28
  226.9 2.4 slice-start
  228.0 2.0 slice-start.1
  (5 other events, 6.6 us)
Sparse Core Ops, SparseCore 0:
  219.0 122.9 all-reduce.4
  345.5 55.1 reduce-scatter.3
